TPU v7x, 32 devices: a whole 2x2x4 slice. The times are simulated.
32 devices in a mesh: row: 2 (over x), col: 16 (over z, y, core).
Axes of the slice: x: 2, y: 2, z: 4, core: 2. Of those that a mesh axis runs over, the one named last changes fastest.
Arguments:
- query_proj: bfloat16 [16384, 4096], P(('col', 'row')), may hold values from -9 to 9
- key_proj: bfloat16 [16384, 512], P(('col', 'row')), may hold values from -9 to 9
- value_proj: bfloat16 [16384, 512], P(('col', 'row')), may hold values from -6 to 6
- segment_ids: int32 [16, 1024], P('col'), may hold values from 0 to 3, never falling along the last dimension, each value on 1 to 512 neighbouring positions
- out_weight: bfloat16 [4096, 8192], P('col', 'row'), may hold values from -0.09375 to 0.09375
- residual: bfloat16 [16384, 8192], P('col', 'row'), may hold values from -4 to 4
- norm_gain: float32 [8192], P('row'), may hold values from 0.1 to 1.9
Outputs:
- residual_sum: bfloat16 [16384, 8192], P('col', 'row')
- normed: bfloat16 [16384, 8192], P('col', 'row')
Inputs may be any that keep to these rules, and one draw needn't show every extreme that they name: `segment_ids`: along each packed sequence the document number never falls; each document spans at most 512 positions and one spans exactly that.
All inputs are finite; a program needn't handle non-finite values.
Results may differ from a plain program's by a relative error of at most 0.0044.
Values may be sent and summed in bfloat16 or wider, within the bound.
A program may use at most 192 MiB of HBM per device.

v0:
```python
import jax
import jax.numpy as jnp
from jax import lax
from jax.sharding import PartitionSpec as P

D = 8192
HD = 128
HK = 4


def attend_local(query_heads, key_heads, value_heads, segment_row):
    length = query_heads.shape[0]
    kv_local = key_heads.shape[1] // HD
    group = query_heads.shape[1] // HD // kv_local
    query_grid = query_heads.reshape(length, kv_local, group, HD).transpose(1, 2, 0, 3)
    key_grid = key_heads.reshape(length, kv_local, HD).transpose(1, 0, 2)
    value_grid = value_heads.reshape(length, kv_local, HD).transpose(1, 0, 2)
    places = jnp.arange(length)
    allowed = (segment_row[:, None] == segment_row[None, :]) & (places[None, :] <= places[:, None])

    def one_group(operands):
        group_query, group_key, group_value = operands
        scores = jnp.einsum(
            "gqd,kd->gqk", group_query, group_key, preferred_element_type=jnp.float32
        ) * HD ** (-0.5)
        scores = jnp.where(allowed, scores, jnp.float32(-1e30))
        peak = jnp.max(scores, axis=-1, keepdims=True)
        weights = jnp.where(allowed, jnp.exp(scores - peak), jnp.float32(0.0))
        totals = jnp.sum(weights, axis=-1, keepdims=True)
        probs = weights.astype(jnp.bfloat16)
        mixture = (
            jnp.einsum("gqk,kd->gqd", probs, group_value, preferred_element_type=jnp.float32)
            / totals
        )
        return mixture.astype(jnp.bfloat16)

    heads_out = lax.map(one_group, (query_grid, key_grid, value_grid))
    return heads_out.transpose(2, 0, 1, 3).reshape(length, kv_local * group * HD)


def widen_heads(proj_rows, repeat):
    rows_local = proj_rows.shape[0]
    kv_count = proj_rows.shape[1] // HD
    if repeat == 1:
        return proj_rows
    spread = jnp.broadcast_to(
        proj_rows.reshape(rows_local, kv_count, 1, HD), (rows_local, kv_count, repeat, HD)
    )
    return spread.reshape(rows_local, kv_count * repeat * HD)


def body(query_proj, key_proj, value_proj, segment_ids, out_weight, residual, norm_gain):
    row_count = lax.axis_size("row")
    repeat = max(row_count // HK, 1)
    key_wide = widen_heads(key_proj, repeat)
    value_wide = widen_heads(value_proj, repeat)
    query_heads, key_heads, value_heads = (
        lax.all_to_all(query_proj, "row", split_axis=1, concat_axis=0, tiled=True),
        lax.all_to_all(key_wide, "row", split_axis=1, concat_axis=0, tiled=True),
        lax.all_to_all(value_wide, "row", split_axis=1, concat_axis=0, tiled=True),
    )
    attn = attend_local(query_heads, key_heads, value_heads, segment_ids[0])
    panel_rows = lax.all_gather(attn, "row", axis=1, tiled=True)
    projected = jnp.dot(
        panel_rows,
        lax.all_gather(out_weight, "col", axis=0, tiled=True),
        preferred_element_type=jnp.float32,
    )
    hidden_sum = residual.astype(jnp.float32) + projected
    squares = lax.psum(jnp.sum(hidden_sum * hidden_sum, axis=1), "row")
    scaled = lax.rsqrt(squares / D + jnp.float32(1e-05))
    normed = hidden_sum * scaled[:, None] * norm_gain[None, :]
    return (hidden_sum.astype(jnp.bfloat16), normed.astype(jnp.bfloat16))


def solution(mesh):
    placed = (
        P(("col", "row"), None),
        P(("col", "row"), None),
        P(("col", "row"), None),
        P("col", None),
        P("col", "row"),
        P("col", "row"),
        P("row"),
    )
    return jax.shard_map(
        body,
        mesh=mesh,
        in_specs=placed,
        out_specs=(P("col", "row"), P("col", "row")),
        check_vma=False,
    )
```

profile of v0, /device:TPU:0, one launch (start us, length us, event | category | flops | bytes accessed | tf_op | source)
XLA Modules:
  0.0 514.9 jit_solution(6233350073334996084)
XLA Ops:
  7.2 1.9 copy.42
  9.0 4.2 all-to-all-start.1
  13.2 1.9 copy.41
  15.1 6.9 %all-to-all-done.1 = bf16[512,2,256]{2,0,1:T(8,128)(2,1)S(1)} async-done(((bf16[512,2,256]{2,0,1:T(8,128)(2,1)}), bf16[512,2,256]{2,0,1:T(8,128)(2,1)S(1)}, u32[]{:S(2)}, u32[]{:S(2)}) %all-to-all-start.1) | async-done | bytes 524320 | tf_op jit(solution)/shard_map/all_to_all | solution.py:59
  22.0 3.5 all-to-all-start.2
  25.5 4.8 copy.40
  30.3 2.9 all-to-all-done.2
  33.1 5.6 %all-to-all-start = ((bf16[512,2,2048]{2,0,1:T(8,128)(2,1)}), bf16[512,2,2048]{2,0,1:T(8,128)(2,1)}, u32[]{:S(2)}, u32[]{:S(2)}) async-start(bf16[512,2,2048]{2,0,1:T(8,128)(2,1)} %bitcast.71), calls=%async_computation | async-start | bytes 8388608 | tf_op jit(solution)/shard_map/all_to_all | solution.py:58
  38.8 0.0 copy-start
  38.8 0.0 all-gather.3.cloned.1.call-start
  38.8 0.1 reshape.34
  39.0 0.9 copy.15
  39.8 0.1 reshape.35
  40.0 0.9 copy.16
  40.9 44.1 %all-to-all-done = bf16[512,2,2048]{2,0,1:T(8,128)(2,1)} async-done(((bf16[512,2,2048]{2,0,1:T(8,128)(2,1)}), bf16[512,2,2048]{2,0,1:T(8,128)(2,1)}, u32[]{:S(2)}, u32[]{:S(2)}) %all-to-all-start) | async-done | bytes 4194336 | tf_op jit(solution)/shard_map/all_to_all | solution.py:58
  85.0 5.6 %copy.25 = bf16[128,8,16,128]{3,2,1,0:T(8,128)(2,1)} copy(bf16[128,8,16,128]{3,1,2,0:T(8,128)(2,1)} %bitcast.23) | data formatting | bytes 8388608
  90.6 0.0 copy-done
  90.6 74.1 %while.11 = (s32[]{:T(128)}, bf16[2,8,1024,128]{2,3,1,0:T(8,128)(2,1)}, bf16[2,8,1024,128]{3,1,0,2:T(8,128)(2,1)}, bf16[2,1024,128]{2,1,0:T(8,128)(2,1)}, bf16[2...) while((s32[]{:T(128)}, bf16[2,8,1024,128]{2,3,1,0:T(8,128)(2,1)}, ...), condition=%wide.region_3.4_spmd.clone, body=%wide.region_0.3_spmd.clone.sunk | while | flops 4350542848 | bytes 54072912 | solution.py:37
  90.6 1.7 constant_dynamic-slice_fusion.2
  92.3 0.6 fusion.52
  92.9 20.1 %fusion.53 = (f32[8,1024]{1,0:T(8,128)S(1)}, bf16[8,1024,1024]{1,2,0:T(8,128)(2,1)}) fusion(pred[1024,1024]{0,1:T(8,128)(4,1)S(1)} %fusion.52, bf16[1,8,1024,128]{3,1,0,2:T(8,128)(2,1)S(1)} %constant_dynamic-slice_fusion.2, bf16[2,1024,128]{2,1,0:T(8,128)(2,1)} %get-tuple-element.134, s32[]{:T(128)} %get-tuple-element.124), kind=kOutput, calls=%fused_computation.37.clone.1 | convolution fusion | flops 2197816320 | bytes 21266944 | tf_op jit(solution)/shard_map/while/body/eval_jaxpr/sub | solution.py:28
  113.1 10.1 %fusion.54 = bf16[1,8,1024,128]{3,2,1,0:T(8,128)(2,1)} fusion(f32[8,1024]{1,0:T(8,128)S(1)} %get-tuple-element.115, bf16[8,1024,1024]{1,2,0:T(8,128)(2,1)} %get-tuple-element.116, bf16[2,1024,128]{2,1,0:T(8,128)(2,1)} %get-tuple-element.135, s32[]{:T(128)} %get-tuple-element.124), kind=kOutput, calls=%fused_computation.16.clone.1 | convolution fusion | flops 2149580800 | bytes 19169792 | tf_op jit(solution)/shard_map/while/body/eval_jaxpr/gqk,kd->gqd/dot_general | solution.py:32
  123.2 2.9 copy.46
  126.0 1.6 constant_dynamic-update-slice_fusion.2
  127.6 1.7 constant_dynamic-slice_fusion.2
  129.4 0.6 fusion.52
  130.0 20.1 %fusion.53 = (f32[8,1024]{1,0:T(8,128)S(1)}, bf16[8,1024,1024]{1,2,0:T(8,128)(2,1)}) fusion(pred[1024,1024]{0,1:T(8,128)(4,1)S(1)} %fusion.52, bf16[1,8,1024,128]{3,1,0,2:T(8,128)(2,1)S(1)} %constant_dynamic-slice_fusion.2, bf16[2,1024,128]{2,1,0:T(8,128)(2,1)} %get-tuple-element.134, s32[]{:T(128)} %get-tuple-element.124), kind=kOutput, calls=%fused_computation.37.clone.1 | convolution fusion | flops 2197816320 | bytes 21266944 | tf_op jit(solution)/shard_map/while/body/eval_jaxpr/sub | solution.py:28
  150.1 10.1 %fusion.54 = bf16[1,8,1024,128]{3,2,1,0:T(8,128)(2,1)} fusion(f32[8,1024]{1,0:T(8,128)S(1)} %get-tuple-element.115, bf16[8,1024,1024]{1,2,0:T(8,128)(2,1)} %get-tuple-element.116, bf16[2,1024,128]{2,1,0:T(8,128)(2,1)} %get-tuple-element.135, s32[]{:T(128)} %get-tuple-element.124), kind=kOutput, calls=%fused_computation.16.clone.1 | convolution fusion | flops 2149580800 | bytes 19169792 | tf_op jit(solution)/shard_map/while/body/eval_jaxpr/gqk,kd->gqd/dot_general | solution.py:32
  160.2 2.9 copy.46
  163.1 1.6 constant_dynamic-update-slice_fusion.2
  164.7 0.0 all-gather.3.cloned.1.call-update
  164.7 0.0 all-gather.5.cloned.1.call-start
  164.8 0.7 all-gather.5.cloned.1.call-update
  165.5 0.0 copy-start.1
  165.5 103.3 %all-gather.3.cloned.1.call-done = bf16[1024,4096]{0,1:T(8,128)(2,1)} async-done(((bf16[1024,2048]{0,1:T(8,128)(2,1)}), bf16[1024,4096]{0,1:T(8,128)(2,1)}) %all-gather.3.cloned.1.call-update) | async-done | bytes 8388624 | tf_op jit(solution)/shard_map/all_gather | solution.py:63
  268.8 169.7 %all-gather.5.cloned.1.call-done = bf16[4096,4096]{1,0:T(8,128)(2,1)} async-done(((bf16[256,4096]{1,0:T(8,128)(2,1)}), bf16[4096,4096]{1,0:T(8,128)(2,1)}) %all-gather.5.cloned.1.call-update) | async-done | bytes 33554448 | tf_op jit(solution)/shard_map/all_gather | solution.py:66
  438.5 45.1 %multiply_reduce_fusion = (f32[1024]{0:T(1024)S(1)}, f32[1024,4096]{1,0:T(8,128)}) fusion(bf16[1024,4096]{0,1:T(8,128)(2,1)} %all-gather.3.cloned.1.call-done, bf16[4096,4096]{1,0:T(8,128)(2,1)} %all-gather.5.cloned.1.call-done, bf16[1024,4096]{1,0:T(8,128)(2,1)} %param.14), kind=kOutput, calls=%fused_computation.31 | convolution fusion | flops 34376515584 | bytes 67112960 | tf_op jit(solution)/shard_map/dot_general | solution.py:64
  483.6 4.9 psum.7
  488.5 0.0 copy-done.1
  488.5 19.5 %multiply_convert_fusion = (bf16[1024,4096]{1,0:T(8,128)(2,1)}, bf16[1024,4096]{1,0:T(8,128)(2,1)}) fusion(f32[1024,4096]{1,0:T(8,128)} %get-tuple-element.73, f32[4096]{0:T(1024)S(1)} %copy-done.1, f32[1024]{0:T(1024)S(1)} %add_rsqrt_fusion), kind=kLoop, calls=%fused_computation.30 | loop fusion | flops 16777216 | bytes 33574912 | tf_op jit(solution)/shard_map/convert_element_type | solution.py:73
  (2 shorter events, 0.0 us)
Async XLA Ops:
  9.0 12.9 %all-to-all-start.1 = ((bf16[512,2,256]{2,0,1:T(8,128)(2,1)}), bf16[512,2,256]{2,0,1:T(8,128)(2,1)S(1)}, u32[]{:S(2)}, u32[]{:S(2)}) async-start(bf16[512,2,256]{2,0,1:T(8,128)(2,1)} %bitcast.59), calls=%async_computation.1 | async-start | bytes 1048576 | tf_op jit(solution)/shard_map/all_to_all | solution.py:59
  22.0 11.2 %all-to-all-start.2 = ((bf16[512,2,256]{2,0,1:T(8,128)(2,1)}), bf16[512,2,256]{2,0,1:T(8,128)(2,1)S(1)}, u32[]{:S(2)}, u32[]{:S(2)}) async-start(bf16[512,2,256]{2,0,1:T(8,128)(2,1)} %bitcast.58), calls=%async_computation.2 | async-start | bytes 1048576 | tf_op jit(solution)/shard_map/all_to_all | solution.py:60
  33.1 51.8 %all-to-all-start = ((bf16[512,2,2048]{2,0,1:T(8,128)(2,1)}), bf16[512,2,2048]{2,0,1:T(8,128)(2,1)}, u32[]{:S(2)}, u32[]{:S(2)}) async-start(bf16[512,2,2048]{2,0,1:T(8,128)(2,1)} %bitcast.71), calls=%async_computation | async-start | bytes 8388608 | tf_op jit(solution)/shard_map/all_to_all | solution.py:58
  38.8 51.8 %copy-start = (s32[1,1024]{1,0:T(1,128)S(1)}, s32[1,1024]{1,0:T(1,128)}, u32[]{:S(2)}) copy-start(s32[1,1024]{1,0:T(1,128)} %param.12) | copy-start | bytes 12292
  38.8 230.0 %all-gather.3.cloned.1.call-start = ((), (), s32[]{:S(2)}) async-start(), calls=%async_computation.3 | async-start | bytes 12582912 | tf_op jit(solution)/shard_map/all_gather | solution.py:63
  164.7 273.8 %all-gather.5.cloned.1.call-start = ((), (), s32[]{:S(2)}) async-start(), calls=%async_computation.4 | async-start | bytes 35651584 | tf_op jit(solution)/shard_map/all_gather | solution.py:66
  165.5 323.1 %copy-start.1 = (f32[4096]{0:T(1024)S(1)}, f32[4096]{0:T(1024)}, u32[]{:S(2)}) copy-start(f32[4096]{0:T(1024)} %param.15) | copy-start | bytes 49156
Sparse Core Ops, SparseCore 0:
  164.9 103.9 all-gather.2
  270.4 168.0 all-gather.4
where the time goes:
time: 516 us; the launch traced here: 515 us
  waiting for transfers between devices  328 us (64%)
  matrix products  106 us (21%)
  local copies, waits for them, and re-layouts  28.5 us (6%)
  other arithmetic  20.7 us (4%)
  between operations  14.1 us (3%)
  starting transfers between devices  13.4 us (3%)
    all_gather x1, waiting for transfers between devices, body(): lax.all_gather(out_weight, 'col', axis=0, tiled=True)  170 us
    all_gather x1, waiting for transfers between devices, body(): panel_rows = lax.all_gather(attn, 'row', axis=1, tiled=True)  103 us
    dot_general x1, matrix products, body(): jnp.dot(panel_rows, lax.all_gather(out_weight, 'col', axis=0, tiled=True)...  45.1 us
    all_to_all x1, waiting for transfers between devices, body(): lax.all_to_all(query_proj, 'row', split_axis=1, concat_axis=0, tiled=True)  44.1 us
    sub x2, matrix products, one_group(): weights = jnp.where(allowed, jnp.exp(scores - peak), jnp.float32(0.0))  40.3 us
    dot_general x2, matrix products, one_group(): jnp.einsum('gqk,kd->gqd', probs, group_value, preferred_element_type=jnp....  20.2 us
    convert_element_type x1, other arithmetic, body(): return (hidden_sum.astype(jnp.bfloat16), normed.astype(jnp.bfloat16))  19.5 us
  transfers between devices with their start and end apart: 5, of which 5 were waited for; matrix products, arithmetic and copies ran while one was open for 2% of the time, Pallas kernels for 0%

commit v1 on v0

--- a/solution.py
+++ b/solution.py
@@ -56,7 +56,12 @@
     value_wide = widen_heads(value_proj, repeat)
     query_heads, key_heads, value_heads = (
         lax.all_to_all(query_proj, "row", split_axis=1, concat_axis=0, tiled=True),
-        lax.all_to_all(key_wide, "row", split_axis=1, concat_axis=0, tiled=True),
+        jnp.concatenate(
+            lax.all_to_all(
+                jnp.stack(jnp.split(key_wide, lax.axis_size("row"), axis=1)), "row", 0, 0
+            ),
+            axis=0,
+        ),
         lax.all_to_all(value_wide, "row", split_axis=1, concat_axis=0, tiled=True),
     )
     attn = attend_local(query_heads, key_heads, value_heads, segment_ids[0])

time: 516 us -> 516 us (level)
  no operation moved by 1% of the time
where the time goes in v1:
time: 516 us; the launch traced here: 515 us
  waiting for transfers between devices  328 us (64%)
  matrix products  106 us (21%)
  local copies, waits for them, and re-layouts  27.7 us (5%)
  other arithmetic  21.6 us (4%)
  between operations  14.1 us (3%)
  starting transfers between devices  13.4 us (3%)
    all_gather x1, waiting for transfers between devices, body(): lax.all_gather(out_weight, 'col', axis=0, tiled=True)  170 us
    all_gather x1, waiting for transfers between devices, body(): panel_rows = lax.all_gather(attn, 'row', axis=1, tiled=True)  103 us
    dot_general x1, matrix products, body(): jnp.dot(panel_rows, lax.all_gather(out_weight, 'col', axis=0, tiled=True)...  45 us
    all_to_all x1, waiting for transfers between devices, body(): lax.all_to_all(query_proj, 'row', split_axis=1, concat_axis=0, tiled=True)  44.1 us
    sub x2, matrix products, one_group(): weights = jnp.where(allowed, jnp.exp(scores - peak), jnp.float32(0.0))  40.3 us
    dot_general x2, matrix products, one_group(): jnp.einsum('gqk,kd->gqd', probs, group_value, preferred_element_type=jnp....  20.2 us
    convert_element_type x1, other arithmetic, body(): return (hidden_sum.astype(jnp.bfloat16), normed.astype(jnp.bfloat16))  19.6 us
  transfers between devices with their start and end apart: 5, of which 5 were waited for; matrix products, arithmetic and copies ran while one was open for 2% of the time, Pallas kernels for 0%

profile of v1, /device:TPU:0, one launch (start us, length us, event | category | flops | bytes accessed | tf_op | source)
XLA Modules:
  0.0 515.0 jit_solution(9314845042968437290)
XLA Ops:
  7.2 1.1 slice_bitcast_fusion.1
  8.2 0.8 pad_maximum_fusion
  9.1 4.2 all-to-all-start.1
  13.3 1.9 copy.38
  15.1 6.9 %all-to-all-done.1 = bf16[2,512,256]{2,1,0:T(8,128)(2,1)S(1)} async-done(((bf16[2,512,256]{2,1,0:T(8,128)(2,1)}), bf16[2,512,256]{2,1,0:T(8,128)(2,1)S(1)}, u32[]{:S(2)}, u32[]{:S(2)}) %all-to-all-start.1) | async-done | bytes 524320 | tf_op jit(solution)/shard_map/all_to_all | solution.py:60
  22.0 3.5 all-to-all-start.2
  25.5 4.8 copy.37
  30.3 2.9 all-to-all-done.2
  33.2 5.6 %all-to-all-start = ((bf16[512,2,2048]{2,0,1:T(8,128)(2,1)}), bf16[512,2,2048]{2,0,1:T(8,128)(2,1)}, u32[]{:S(2)}, u32[]{:S(2)}) async-start(bf16[512,2,2048]{2,0,1:T(8,128)(2,1)} %bitcast.70), calls=%async_computation | async-start | bytes 8388608 | tf_op jit(solution)/shard_map/all_to_all | solution.py:58
  38.8 0.0 copy-start
  38.8 0.0 all-gather.3.cloned.1.call-start
  38.9 0.1 reshape_reshape.3
  39.0 0.9 copy.14
  39.9 0.1 reshape.27
  40.0 0.9 copy.15
  40.9 44.1 %all-to-all-done = bf16[512,2,2048]{2,0,1:T(8,128)(2,1)} async-done(((bf16[512,2,2048]{2,0,1:T(8,128)(2,1)}), bf16[512,2,2048]{2,0,1:T(8,128)(2,1)}, u32[]{:S(2)}, u32[]{:S(2)}) %all-to-all-start) | async-done | bytes 4194336 | tf_op jit(solution)/shard_map/all_to_all | solution.py:58
  85.0 5.6 %copy.23 = bf16[128,8,16,128]{3,2,1,0:T(8,128)(2,1)} copy(bf16[128,8,16,128]{3,1,2,0:T(8,128)(2,1)} %bitcast.22) | data formatting | bytes 8388608
  90.6 0.0 copy-done
  90.6 74.1 %while.11 = (s32[]{:T(128)}, bf16[2,8,1024,128]{2,3,1,0:T(8,128)(2,1)}, bf16[2,8,1024,128]{3,1,0,2:T(8,128)(2,1)}, bf16[2,1024,128]{2,1,0:T(8,128)(2,1)}, bf16[2...) while((s32[]{:T(128)}, bf16[2,8,1024,128]{2,3,1,0:T(8,128)(2,1)}, ...), condition=%wide.region_3.4_spmd.clone, body=%wide.region_0.3_spmd.clone.sunk | while | flops 4350542848 | bytes 54072912 | solution.py:37
  90.6 1.7 constant_dynamic-slice_fusion.2
  92.4 0.6 fusion.52
  93.0 20.1 %fusion.53 = (f32[8,1024]{1,0:T(8,128)S(1)}, bf16[8,1024,1024]{1,2,0:T(8,128)(2,1)}) fusion(pred[1024,1024]{0,1:T(8,128)(4,1)S(1)} %fusion.52, bf16[1,8,1024,128]{3,1,0,2:T(8,128)(2,1)S(1)} %constant_dynamic-slice_fusion.2, bf16[2,1024,128]{2,1,0:T(8,128)(2,1)} %get-tuple-element.136, s32[]{:T(128)} %get-tuple-element.126), kind=kOutput, calls=%fused_computation.39.clone.1 | convolution fusion | flops 2197816320 | bytes 21266944 | tf_op jit(solution)/shard_map/while/body/eval_jaxpr/sub | solution.py:28
  113.1 10.1 %fusion.54 = bf16[1,8,1024,128]{3,2,1,0:T(8,128)(2,1)} fusion(f32[8,1024]{1,0:T(8,128)S(1)} %get-tuple-element.117, bf16[8,1024,1024]{1,2,0:T(8,128)(2,1)} %get-tuple-element.118, bf16[2,1024,128]{2,1,0:T(8,128)(2,1)} %get-tuple-element.137, s32[]{:T(128)} %get-tuple-element.126), kind=kOutput, calls=%fused_computation.16.clone.1 | convolution fusion | flops 2149580800 | bytes 19169792 | tf_op jit(solution)/shard_map/while/body/eval_jaxpr/gqk,kd->gqd/dot_general | solution.py:32
  123.2 2.9 copy.42
  126.1 1.6 constant_dynamic-update-slice_fusion.2
  127.7 1.7 constant_dynamic-slice_fusion.2
  129.4 0.6 fusion.52
  130.0 20.2 %fusion.53 = (f32[8,1024]{1,0:T(8,128)S(1)}, bf16[8,1024,1024]{1,2,0:T(8,128)(2,1)}) fusion(pred[1024,1024]{0,1:T(8,128)(4,1)S(1)} %fusion.52, bf16[1,8,1024,128]{3,1,0,2:T(8,128)(2,1)S(1)} %constant_dynamic-slice_fusion.2, bf16[2,1024,128]{2,1,0:T(8,128)(2,1)} %get-tuple-element.136, s32[]{:T(128)} %get-tuple-element.126), kind=kOutput, calls=%fused_computation.39.clone.1 | convolution fusion | flops 2197816320 | bytes 21266944 | tf_op jit(solution)/shard_map/while/body/eval_jaxpr/sub | solution.py:28
  150.2 10.1 %fusion.54 = bf16[1,8,1024,128]{3,2,1,0:T(8,128)(2,1)} fusion(f32[8,1024]{1,0:T(8,128)S(1)} %get-tuple-element.117, bf16[8,1024,1024]{1,2,0:T(8,128)(2,1)} %get-tuple-element.118, bf16[2,1024,128]{2,1,0:T(8,128)(2,1)} %get-tuple-element.137, s32[]{:T(128)} %get-tuple-element.126), kind=kOutput, calls=%fused_computation.16.clone.1 | convolution fusion | flops 2149580800 | bytes 19169792 | tf_op jit(solution)/shard_map/while/body/eval_jaxpr/gqk,kd->gqd/dot_general | solution.py:32
  160.3 2.9 copy.42
  163.1 1.6 constant_dynamic-update-slice_fusion.2
  164.8 0.0 all-gather.3.cloned.1.call-update
  164.8 0.0 all-gather.5.cloned.1.call-start
  164.8 0.7 all-gather.5.cloned.1.call-update
  165.5 0.0 copy-start.1
  165.5 103.3 %all-gather.3.cloned.1.call-done = bf16[1024,4096]{0,1:T(8,128)(2,1)} async-done(((bf16[1024,2048]{0,1:T(8,128)(2,1)}), bf16[1024,4096]{0,1:T(8,128)(2,1)}) %all-gather.3.cloned.1.call-update) | async-done | bytes 8388624 | tf_op jit(solution)/shard_map/all_gather | solution.py:68
  268.9 169.7 %all-gather.5.cloned.1.call-done = bf16[4096,4096]{1,0:T(8,128)(2,1)} async-done(((bf16[256,4096]{1,0:T(8,128)(2,1)}), bf16[4096,4096]{1,0:T(8,128)(2,1)}) %all-gather.5.cloned.1.call-update) | async-done | bytes 33554448 | tf_op jit(solution)/shard_map/all_gather | solution.py:71
  438.6 45.0 %multiply_reduce_fusion = (f32[1024]{0:T(1024)S(1)}, f32[1024,4096]{1,0:T(8,128)}) fusion(bf16[1024,4096]{0,1:T(8,128)(2,1)} %all-gather.3.cloned.1.call-done, bf16[4096,4096]{1,0:T(8,128)(2,1)} %all-gather.5.cloned.1.call-done, bf16[1024,4096]{1,0:T(8,128)(2,1)} %param.14), kind=kOutput, calls=%fused_computation.31 | convolution fusion | flops 34376515584 | bytes 67112960 | tf_op jit(solution)/shard_map/dot_general | solution.py:69
  483.6 4.9 psum.7
  488.5 0.0 copy-done.1
  488.5 19.6 %multiply_convert_fusion = (bf16[1024,4096]{1,0:T(8,128)(2,1)}, bf16[1024,4096]{1,0:T(8,128)(2,1)}) fusion(f32[1024,4096]{1,0:T(8,128)} %get-tuple-element.75, f32[4096]{0:T(1024)S(1)} %copy-done.1, f32[1024]{0:T(1024)S(1)} %add_rsqrt_fusion), kind=kLoop, calls=%fused_computation.30 | loop fusion | flops 16777216 | bytes 33574912 | tf_op jit(solution)/shard_map/convert_element_type | solution.py:78
  (2 shorter events, 0.0 us)
Async XLA Ops:
  9.1 12.9 %all-to-all-start.1 = ((bf16[2,512,256]{2,1,0:T(8,128)(2,1)}), bf16[2,512,256]{2,1,0:T(8,128)(2,1)S(1)}, u32[]{:S(2)}, u32[]{:S(2)}) async-start(bf16[2,512,256]{2,1,0:T(8,128)(2,1)} %pad_maximum_fusion), calls=%async_computation.1 | async-start | bytes 1048576 | tf_op jit(solution)/shard_map/all_to_all | solution.py:60
  22.0 11.2 %all-to-all-start.2 = ((bf16[512,2,256]{2,0,1:T(8,128)(2,1)}), bf16[512,2,256]{2,0,1:T(8,128)(2,1)S(1)}, u32[]{:S(2)}, u32[]{:S(2)}) async-start(bf16[512,2,256]{2,0,1:T(8,128)(2,1)} %bitcast.58), calls=%async_computation.2 | async-start | bytes 1048576 | tf_op jit(solution)/shard_map/all_to_all | solution.py:65
  33.2 51.8 %all-to-all-start = ((bf16[512,2,2048]{2,0,1:T(8,128)(2,1)}), bf16[512,2,2048]{2,0,1:T(8,128)(2,1)}, u32[]{:S(2)}, u32[]{:S(2)}) async-start(bf16[512,2,2048]{2,0,1:T(8,128)(2,1)} %bitcast.70), calls=%async_computation | async-start | bytes 8388608 | tf_op jit(solution)/shard_map/all_to_all | solution.py:58
  38.8 51.8 %copy-start = (s32[1,1024]{1,0:T(1,128)S(1)}, s32[1,1024]{1,0:T(1,128)}, u32[]{:S(2)}) copy-start(s32[1,1024]{1,0:T(1,128)} %param.12) | copy-start | bytes 12292
  38.8 230.1 %all-gather.3.cloned.1.call-start = ((), (), s32[]{:S(2)}) async-start(), calls=%async_computation.3 | async-start | bytes 12582912 | tf_op jit(solution)/shard_map/all_gather | solution.py:68
  164.8 273.8 %all-gather.5.cloned.1.call-start = ((), (), s32[]{:S(2)}) async-start(), calls=%async_computation.4 | async-start | bytes 35651584 | tf_op jit(solution)/shard_map/all_gather | solution.py:71
  165.5 323.0 %copy-start.1 = (f32[4096]{0:T(1024)S(1)}, f32[4096]{0:T(1024)}, u32[]{:S(2)}) copy-start(f32[4096]{0:T(1024)} %param.15) | copy-start | bytes 49156
Sparse Core Ops, SparseCore 0:
  164.9 103.9 all-gather.2
  270.5 168.0 all-gather.4
